TPU v7x, 32 devices: a whole 2x2x4 slice. The times are simulated.
32 devices in a mesh: dp: 8 (over z, x), tensor: 4 (over y, core).
Axes of the slice: x: 2, y: 2, z: 4, core: 2. Of those that a mesh axis runs over, the one named last changes fastest.
Arguments:
- tokens: bfloat16 [8192, 2048], P(('dp', 'tensor')), may hold values from -6 to 6
- pieces: int32 [8192], P('dp'), may hold values from 0 to 32, as said below
- positions: int32 [8192], P('dp'), may hold values from 0 to 798, as said below
- cotangent: bfloat16 [8192, 2048], P(('dp', 'tensor')), may hold values from -6 to 6
- attn_norm: float32 [2048], P('dp'), may hold values from 0.25 to 1.75
- w_query: float32 [2048, 2048], P('dp', 'tensor'), may hold values from -0.125 to 0.125
- w_key: float32 [2048, 512], P('dp', 'tensor'), may hold values from -0.125 to 0.125
- w_value: float32 [2048, 512], P('dp', 'tensor'), may hold values from -0.125 to 0.125
- w_out: float32 [2048, 2048], P('tensor', 'dp'), may hold values from -0.75 to 0.75
- mlp_norm: float32 [2048], P('dp'), may hold values from 0.25 to 1.75
- w_gate: float32 [2048, 8192], P('dp', 'tensor'), may hold values from -0.125 to 0.125
- w_up: float32 [2048, 8192], P('dp', 'tensor'), may hold values from -0.125 to 0.125
- w_down: float32 [8192, 2048], P('tensor', 'dp'), may hold values from -0.0625 to 0.0625
Outputs:
- output: bfloat16 [8192, 2048], P(('dp', 'tensor'))
- input_grad: float32 [8192, 2048], P(('dp', 'tensor'))
- grad_attn_norm: float32 [2048], P('dp')
- grad_w_query: float32 [2048, 2048], P('dp', 'tensor')
- grad_w_key: float32 [2048, 512], P('dp', 'tensor')
- grad_w_value: float32 [2048, 512], P('dp', 'tensor')
- grad_w_out: float32 [2048, 2048], P('tensor', 'dp')
- grad_mlp_norm: float32 [2048], P('dp')
- grad_w_gate: float32 [2048, 8192], P('dp', 'tensor')
- grad_w_up: float32 [2048, 8192], P('dp', 'tensor')
- grad_w_down: float32 [8192, 2048], P('tensor', 'dp')
Inputs may be any that keep to these rules, and one draw needn't show every extreme that they name: `pieces`: each aligned run of 256 tokens is text (0) or one picture piece numbered 1 + the run's index among all runs; the last run of every sequence is a picture piece. `positions`: A text token's position is its index within its sequence of 1024 tokens; the t-th token of a picture piece takes the index of the piece's first token + t // 16 + t % 16.
All inputs are finite; a program needn't handle non-finite values.
Results may differ from a plain program's by a relative error of at most 0.02.
Values may be sent and summed in bfloat16 or wider, within the bound.
No kernel may reach another device: no remote copies, remote signals or barrier semaphores. Data moves between devices by JAX's collectives and lax.ppermute only.
A program may use at most 256 MiB of HBM per device.

v0:
```python
from functools import reduce
import math
import jax
import jax.numpy as jnp
from jax import lax
from jax.sharding import PartitionSpec as P

HEADS = 32
KV_HEADS = 8
HEAD_DIM = 64


def rotary_angles(positions, head_size):
    half = head_size // 2
    base = jnp.power(500000.0, -(jnp.arange(half, dtype=jnp.float32) * 2.0 / head_size))
    wavelen = 2.0 * math.pi / base
    smooth = (8192.0 / wavelen - 1.0) / 3.0
    blended = (1.0 - smooth) * base / 32.0 + smooth * base
    scaled = jnp.where(wavelen > 8192.0, base / 32.0, jnp.where(wavelen < 2048.0, base, blended))
    return positions.astype(jnp.float32)[:, None] * scaled[None, :]


def rotate(field, angles):
    half = field.shape[-1] // 2
    cosine = jnp.cos(angles)[:, None, :]
    sine = jnp.sin(angles)[:, None, :]
    first = field[..., :half]
    second = field[..., half:]
    return jnp.concatenate(
        [first * cosine - second * sine, second * cosine + first * sine], axis=-1
    )


def normalize(residual, gain):
    inverse = lax.rsqrt(jnp.mean(residual * residual, axis=-1, keepdims=True) + 1e-05)
    return ((residual * inverse * gain.astype(jnp.float32)).astype(jnp.bfloat16), inverse)


def normalize_back(grad_normed, residual, inverse, gain):
    scaled = residual * inverse
    grad_gain = jnp.sum(grad_normed * scaled, axis=0)
    weighted = grad_normed * gain.astype(jnp.float32)
    grad_residual = inverse * (
        weighted - scaled * jnp.mean(weighted * scaled, axis=-1, keepdims=True)
    )
    return (grad_residual, grad_gain)


def row_product(left, right):
    return jnp.dot(left, right, preferred_element_type=jnp.float32)


def back_product(lefts, rights):
    parts = [
        lax.dot_general(left, right, (((1,), (1,)), ((), ())), preferred_element_type=jnp.float32)
        for left, right in zip(lefts, rights)
    ]
    return reduce(jnp.add, parts)


def across_rows(left, right):
    return lax.dot_general(
        left, right, (((0,), (0,)), ((), ())), preferred_element_type=jnp.float32
    )


def masked_scores(block_query, keys, pieces, first, scale_factor):
    count = block_query.shape[0]
    length = keys.shape[0]
    scores = (
        jnp.einsum("qgrd,kgd->grqk", block_query, keys, preferred_element_type=jnp.float32)
        * scale_factor
    )
    rows = first + jnp.arange(count)[:, None]
    columns = jnp.arange(length)[None, :]
    owner = pieces[first : first + count][:, None]
    allowed = (columns <= rows) | (owner == pieces[None, :]) & (owner != 0)
    return jnp.where(allowed, scores, -1e30)


def attend(query, keys, values, pieces, scale_factor):
    length = query.shape[0]
    block = min(512, length)
    attended_parts = []
    total_parts = []
    for first in range(0, length, block):
        scores = masked_scores(query[first : first + block], keys, pieces, first, scale_factor)
        peak = jnp.max(scores, axis=-1, keepdims=True)
        exponent = jnp.exp(scores - peak)
        total = jnp.sum(exponent, axis=-1, keepdims=True)
        probs = (exponent / total).astype(jnp.bfloat16)
        attended_parts.append(
            jnp.einsum("grqk,kgd->qgrd", probs, values, preferred_element_type=jnp.float32).astype(
                jnp.bfloat16
            )
        )
        total_parts.append(peak + jnp.log(total))
    return (jnp.concatenate(attended_parts, axis=0), jnp.concatenate(total_parts, axis=2))


def attend_back(query, keys, values, grad_attended, log_totals, pieces, scale_factor):
    length = query.shape[0]
    block = min(512, length)
    grad_query_parts = []
    grad_keys = jnp.zeros(keys.shape, jnp.float32)
    grad_values = jnp.zeros(values.shape, jnp.float32)
    for first in range(0, length, block):
        block_query = query[first : first + block]
        block_grad = grad_attended[first : first + block]
        scores = masked_scores(block_query, keys, pieces, first, scale_factor)
        probs = jnp.exp(scores - log_totals[:, :, first : first + block])
        probs_low = probs.astype(jnp.bfloat16)
        grad_probs = jnp.einsum(
            "qgrd,kgd->grqk", block_grad, values, preferred_element_type=jnp.float32
        )
        inner = jnp.sum(probs * grad_probs, axis=-1, keepdims=True)
        grad_scores = (probs * (grad_probs - inner)).astype(jnp.bfloat16)
        grad_query_parts.append(
            jnp.einsum("grqk,kgd->qgrd", grad_scores, keys, preferred_element_type=jnp.float32)
            * scale_factor
        )
        grad_keys = (
            grad_keys
            + jnp.einsum(
                "grqk,qgrd->kgd", grad_scores, block_query, preferred_element_type=jnp.float32
            )
            * scale_factor
        )
        grad_values = grad_values + jnp.einsum(
            "grqk,qgrd->kgd", probs_low, block_grad, preferred_element_type=jnp.float32
        )
    return (jnp.concatenate(grad_query_parts, axis=0), grad_keys, grad_values)


def gather_rows(rows):
    return lax.all_gather(rows, "tensor", axis=0, tiled=True)


def gather_grads(rows):
    return lax.all_gather(rows, "tensor", axis=0, tiled=True)


def local(
    tokens,
    pieces,
    positions,
    cotangent,
    attn_norm,
    w_query,
    w_key,
    w_value,
    w_out,
    mlp_norm,
    w_gate,
    w_up,
    w_down,
):
    attn_gain, query_weight, key_weight, value_weight, out_weight = (
        lax.all_gather(attn_norm.astype(jnp.bfloat16), "dp", axis=0, tiled=True),
        lax.all_gather(w_query.astype(jnp.bfloat16), "dp", axis=0, tiled=True),
        lax.all_gather(w_key.astype(jnp.bfloat16), "dp", axis=0, tiled=True),
        lax.all_gather(w_value.astype(jnp.bfloat16), "dp", axis=0, tiled=True),
        lax.all_gather(w_out.astype(jnp.bfloat16), "dp", axis=1, tiled=True),
    )
    mlp_gain, gate_weight, up_weight, down_weight = (
        lax.all_gather(mlp_norm.astype(jnp.bfloat16), "dp", axis=0, tiled=True),
        lax.all_gather(w_gate.astype(jnp.bfloat16), "dp", axis=0, tiled=True),
        lax.all_gather(w_up.astype(jnp.bfloat16), "dp", axis=0, tiled=True),
        lax.all_gather(w_down.astype(jnp.bfloat16), "dp", axis=1, tiled=True),
    )
    group = HEADS // KV_HEADS
    key_heads = key_weight.shape[1] // HEAD_DIM
    scale_factor = HEAD_DIM ** (-0.5)
    residual = tokens.astype(jnp.float32)
    normed_one, inverse_one = normalize(residual, attn_gain)
    normed_full = gather_rows(normed_one)
    length = normed_full.shape[0]
    angles = rotary_angles(positions, HEAD_DIM)
    query = jnp.dot(normed_full, query_weight, preferred_element_type=jnp.float32).reshape(
        length, -1, HEAD_DIM
    )
    query = rotate(query, angles).astype(jnp.bfloat16).reshape(length, key_heads, group, HEAD_DIM)
    keys = jnp.dot(normed_full, key_weight, preferred_element_type=jnp.float32).reshape(
        length, key_heads, HEAD_DIM
    )
    keys = rotate(keys, angles).astype(jnp.bfloat16)
    values = jnp.dot(normed_full, value_weight, preferred_element_type=jnp.float32).astype(
        jnp.bfloat16
    )
    values = values.reshape(length, key_heads, HEAD_DIM)
    attended, log_totals = attend(query, keys, values, pieces, scale_factor)
    attended_flat = attended.reshape(length, -1)
    middle = residual + lax.psum_scatter(
        row_product(attended_flat, out_weight), "tensor", scatter_dimension=0, tiled=True
    )
    normed_two, inverse_two = normalize(middle, mlp_gain)
    normed_full_two = gather_rows(normed_two)
    gate = jnp.dot(normed_full_two, gate_weight, preferred_element_type=jnp.float32)
    up = jnp.dot(normed_full_two, up_weight, preferred_element_type=jnp.float32)
    gate_sigmoid = jax.nn.sigmoid(gate)
    activated = gate * gate_sigmoid
    hidden = (activated * up).astype(jnp.bfloat16)
    result = middle + lax.psum_scatter(
        row_product(hidden, down_weight).astype(jnp.bfloat16),
        "tensor",
        scatter_dimension=0,
        tiled=True,
    ).astype(jnp.float32)
    output = result.astype(jnp.bfloat16)
    mlp_gain, gate_weight, up_weight, down_weight = (
        lax.all_gather(mlp_norm.astype(jnp.bfloat16), "dp", axis=0, tiled=True),
        lax.all_gather(w_gate.astype(jnp.bfloat16), "dp", axis=0, tiled=True),
        lax.all_gather(w_up.astype(jnp.bfloat16), "dp", axis=0, tiled=True),
        lax.all_gather(w_down.astype(jnp.bfloat16), "dp", axis=1, tiled=True),
    )
    grad_out = cotangent.astype(jnp.float32)
    grad_out_full = gather_grads(cotangent)
    grad_hidden = lax.dot_general(
        grad_out_full, down_weight, (((1,), (1,)), ((), ())), preferred_element_type=jnp.float32
    )
    grad_gate = (grad_hidden * up * gate_sigmoid * (1.0 + gate * (1.0 - gate_sigmoid))).astype(
        jnp.bfloat16
    )
    grad_up = (grad_hidden * activated).astype(jnp.bfloat16)
    grad_w_down = across_rows(hidden, grad_out_full)
    grad_w_gate = across_rows(normed_full_two, grad_gate)
    grad_w_up = across_rows(normed_full_two, grad_up)
    grad_normed_two = lax.psum_scatter(
        back_product((grad_gate, grad_up), (gate_weight, up_weight)),
        "tensor",
        scatter_dimension=0,
        tiled=True,
    )
    grad_middle_norm, grad_gain_two = normalize_back(grad_normed_two, middle, inverse_two, mlp_gain)
    grad_middle = grad_out + grad_middle_norm
    gain_two_part, grad_w_gate, grad_w_up, grad_w_down = (
        lax.psum_scatter(
            grad_gain_two.astype(jnp.bfloat16), "dp", scatter_dimension=0, tiled=True
        ).astype(jnp.float32),
        lax.psum_scatter(
            grad_w_gate.astype(jnp.bfloat16), "dp", scatter_dimension=0, tiled=True
        ).astype(jnp.float32),
        lax.psum_scatter(
            grad_w_up.astype(jnp.bfloat16), "dp", scatter_dimension=0, tiled=True
        ).astype(jnp.float32),
        lax.psum_scatter(
            grad_w_down.astype(jnp.bfloat16), "dp", scatter_dimension=1, tiled=True
        ).astype(jnp.float32),
    )
    grad_branch_full = gather_grads(grad_middle.astype(jnp.bfloat16))
    attn_gain, query_weight, key_weight, value_weight, out_weight = (
        lax.all_gather(attn_norm.astype(jnp.bfloat16), "dp", axis=0, tiled=True),
        lax.all_gather(w_query.astype(jnp.bfloat16), "dp", axis=0, tiled=True),
        lax.all_gather(w_key.astype(jnp.bfloat16), "dp", axis=0, tiled=True),
        lax.all_gather(w_value.astype(jnp.bfloat16), "dp", axis=0, tiled=True),
        lax.all_gather(w_out.astype(jnp.bfloat16), "dp", axis=1, tiled=True),
    )
    grad_attended = lax.dot_general(
        grad_branch_full, out_weight, (((1,), (1,)), ((), ())), preferred_element_type=jnp.float32
    )
    grad_attended = grad_attended.astype(jnp.bfloat16).reshape(length, key_heads, group, HEAD_DIM)
    grad_query_rot, grad_keys_rot, grad_values = attend_back(
        query, keys, values, grad_attended, log_totals, pieces, scale_factor
    )
    grad_query = (
        rotate(grad_query_rot.reshape(length, -1, HEAD_DIM), -angles)
        .astype(jnp.bfloat16)
        .reshape(length, -1)
    )
    grad_keys = rotate(grad_keys_rot, -angles).astype(jnp.bfloat16).reshape(length, -1)
    grad_values = grad_values.astype(jnp.bfloat16).reshape(length, -1)
    grad_normed_one = lax.psum_scatter(
        back_product(
            (grad_query, grad_keys, grad_values), (query_weight, key_weight, value_weight)
        ).astype(jnp.bfloat16),
        "tensor",
        scatter_dimension=0,
        tiled=True,
    ).astype(jnp.float32)
    grad_input_norm, grad_gain_one = normalize_back(
        grad_normed_one, residual, inverse_one, attn_gain
    )
    input_grad = grad_middle + grad_input_norm
    grad_w_out = across_rows(attended_flat, grad_branch_full)
    grad_w_query = across_rows(normed_full, grad_query)
    grad_w_key = across_rows(normed_full, grad_keys)
    grad_w_value = across_rows(normed_full, grad_values)
    gain_one_part, grad_w_query, grad_w_key, grad_w_value, grad_w_out = (
        lax.psum_scatter(
            grad_gain_one.astype(jnp.bfloat16), "dp", scatter_dimension=0, tiled=True
        ).astype(jnp.float32),
        lax.psum_scatter(
            grad_w_query.astype(jnp.bfloat16), "dp", scatter_dimension=0, tiled=True
        ).astype(jnp.float32),
        lax.psum_scatter(
            grad_w_key.astype(jnp.bfloat16), "dp", scatter_dimension=0, tiled=True
        ).astype(jnp.float32),
        lax.psum_scatter(
            grad_w_value.astype(jnp.bfloat16), "dp", scatter_dimension=0, tiled=True
        ).astype(jnp.float32),
        lax.psum_scatter(
            grad_w_out.astype(jnp.bfloat16), "dp", scatter_dimension=1, tiled=True
        ).astype(jnp.float32),
    )
    gain_one, gain_two = lax.psum((gain_one_part, gain_two_part), "tensor")
    return (
        output,
        input_grad,
        gain_one,
        grad_w_query,
        grad_w_key,
        grad_w_value,
        grad_w_out,
        gain_two,
        grad_w_gate,
        grad_w_up,
        grad_w_down,
    )


def solution(mesh):
    return jax.shard_map(
        local,
        mesh=mesh,
        in_specs=(
            P(("dp", "tensor"), None),
            P("dp"),
            P("dp"),
            P(("dp", "tensor"), None),
            P("dp"),
            P("dp", "tensor"),
            P("dp", "tensor"),
            P("dp", "tensor"),
            P("tensor", "dp"),
            P("dp"),
            P("dp", "tensor"),
            P("dp", "tensor"),
            P("tensor", "dp"),
        ),
        out_specs=(
            P(("dp", "tensor"), None),
            P(("dp", "tensor"), None),
            P("dp"),
            P("dp", "tensor"),
            P("dp", "tensor"),
            P("dp", "tensor"),
            P("tensor", "dp"),
            P("dp"),
            P("dp", "tensor"),
            P("dp", "tensor"),
            P("tensor", "dp"),
        ),
        check_vma=False,
    )
```

profile of v0, /device:TPU:0, one launch (start us, length us, event | category | flops | bytes accessed | tf_op | source)
XLA Modules:
  0.0 1690.8 jit_solution(2839369991846664020)
XLA Ops:
  9.6 22.3 %all-gather = bf16[8,1,256]{2,1,0:T(2,128)(2,1)S(1)} all-gather(bf16[1,1,256]{2,1,0:T(2,128)(2,1)S(1)} %reshape.227), channel_id=1, replica_groups=mesh['dp'=8,'tensor'=4] {'dp'}, dimensions={0}, use_global_device_ids=true | all-gather | bytes 4608 | tf_op jit(solution)/shard_map/all_gather | solution.py:159
  36.8 31.5 %all_gather.50 = bf16[2048,128]{1,0:T(8,128)(2,1)S(1)} all-gather(bf16[256,128]{1,0:T(8,128)(2,1)S(1)} %convert_element_type.198), channel_id=1, replica_groups=mesh['dp'=8,'tensor'=4] {'dp'}, dimensions={0}, use_global_device_ids=true | all-gather | bytes 589824 | tf_op jit(solution)/shard_map/all_gather | solution.py:162
  68.3 32.4 %all_gather.51 = bf16[2048,128]{1,0:T(8,128)(2,1)S(1)} all-gather(bf16[256,128]{1,0:T(8,128)(2,1)S(1)} %convert_element_type.200), channel_id=1, replica_groups=mesh['dp'=8,'tensor'=4] {'dp'}, dimensions={0}, use_global_device_ids=true | all-gather | bytes 589824 | tf_op jit(solution)/shard_map/all_gather | solution.py:161
  107.3 12.4 all-gather.14.cloned.1.call-done
  125.4 7.4 fusion.59
  132.8 8.3 fusion.7
  142.7 7.5 fusion.46
  150.2 7.5 fusion.60
  157.7 8.1 fusion.6
  165.9 7.4 fusion.45
  173.5 7.7 fusion.63
  184.0 18.3 %all-gather.1 = bf16[8,1,256]{2,1,0:T(2,128)(2,1)S(1)} all-gather(bf16[1,1,256]{2,1,0:T(2,128)(2,1)S(1)} %reshape.229), channel_id=1, replica_groups=mesh['dp'=8,'tensor'=4] {'dp'}, dimensions={0}, use_global_device_ids=true | all-gather | bytes 4608 | tf_op jit(solution)/shard_map/all_gather | solution.py:166
  202.3 49.1 %reduce-scatter.12.cloned.1.call-done = f32[256,2048]{1,0:T(8,128)} async-done(((f32[1024,2048]{1,0:T(8,128)}), f32[256,2048]{1,0:T(8,128)}) %reduce-scatter.12.cloned.1.call-update) | async-done | bytes 2097168 | tf_op jit(solution)/shard_map/reduce_scatter | solution.py:193
  261.2 117.3 %all-gather.22.cloned.1.call-done = bf16[2048,2048]{1,0:T(8,128)(2,1)} async-done(((bf16[256,2048]{1,0:T(8,128)(2,1)}), bf16[2048,2048]{1,0:T(8,128)(2,1)}) %all-gather.22.cloned.1.call-update) | async-done | bytes 8388624 | tf_op jit(solution)/shard_map/all_gather | solution.py:168
  378.5 34.7 %all-gather.18.cloned.1.call-done = bf16[1024,2048]{1,0:T(8,128)(2,1)} async-done(((bf16[256,2048]{1,0:T(8,128)(2,1)}), bf16[1024,2048]{1,0:T(8,128)(2,1)}) %all-gather.18.cloned.1.call-update) | async-done | bytes 4194320 | tf_op jit(solution)/shard_map/all_gather | solution.py:136
  413.1 14.7 fusion.65
  427.9 112.4 %all-gather.20.cloned.1.call-done = bf16[2048,2048]{1,0:T(8,128)(2,1)} async-done(((bf16[256,2048]{1,0:T(8,128)(2,1)}), bf16[2048,2048]{1,0:T(8,128)(2,1)}) %all-gather.20.cloned.1.call-update) | async-done | bytes 8388624 | tf_op jit(solution)/shard_map/all_gather | solution.py:167
  540.3 14.5 fusion.64
  554.9 19.7 %all-gather.26.cloned.1.call-done = bf16[1024,2048]{1,0:T(8,128)(2,1)} async-done(((bf16[256,2048]{1,0:T(8,128)(2,1)}), bf16[1024,2048]{1,0:T(8,128)(2,1)}) %all-gather.26.cloned.1.call-update) | async-done | bytes 4194320 | tf_op jit(solution)/shard_map/all_gather | solution.py:140
  574.6 127.6 %all-gather.24.cloned.1.call-done = bf16[2048,2048]{1,0:T(8,128)(2,1)} async-done(((bf16[2048,256]{1,0:T(8,128)(2,1)}), bf16[2048,2048]{1,0:T(8,128)(2,1)}) %all-gather.24.cloned.1.call-update) | async-done | bytes 8388624 | tf_op jit(solution)/shard_map/all_gather | solution.py:169
  702.2 21.9 %multiply_convert_fusion = (bf16[1024,2048]{1,0:T(8,128)(2,1)}, bf16[1024,2048]{1,0:T(8,128)(2,1)}, bf16[1024,2048]{1,0:T(8,128)(2,1)}) fusion(f32[1024,2048]{1,0:T(8,128)} %fusion.64, f32[1024,2048]{1,0:T(8,128)} %fusion.65, bf16[1024,2048]{1,0:T(8,128)(2,1)} %all-gather.26.cloned.1.call-done, bf16[2048,2048]{1,0:T(8,128)(2,1)} %all-gather.24.cloned.1.call-done), kind=kOutput, calls=%fused_computation.27 | convolution fusion | flops 8621391872 | bytes 41943040 | tf_op jit(solution)/shard_map/dot_general | solution.py:218
  724.0 13.1 fusion.66
  737.2 13.6 convolution_add_fusion
  750.9 69.7 %reduce-scatter.16.cloned.1.call-done = f32[256,2048]{1,0:T(8,128)} async-done(((f32[1024,2048]{1,0:T(8,128)}), f32[256,2048]{1,0:T(8,128)}) %reduce-scatter.16.cloned.1.call-update) | async-done | bytes 2097168 | tf_op jit(solution)/shard_map/reduce_scatter | solution.py:228
  825.7 14.3 convolution_convert_fusion.1
  840.1 14.1 convolution_convert_fusion.2
  854.3 14.2 convolution_convert_fusion
  870.2 5.3 convolution_convert_fusion.8
  876.4 10.1 fusion.36
  886.5 5.3 fusion.50
  894.8 15.3 fusion
  910.1 12.2 fusion.2
  928.3 7.6 fusion.3
  936.0 12.2 fusion.5
  955.9 5.9 convolution_convert_fusion.4
  986.2 13.9 convolution_convert_fusion.3
  1002.1 9.3 reduce-scatter.30.cloned.1.call-done
  1014.2 147.4 %reduce-scatter.28.cloned.1.call-done = bf16[256,2048]{1,0:T(8,128)(2,1)} async-done(((bf16[2048,2048]{1,0:T(8,128)(2,1)}), bf16[256,2048]{1,0:T(8,128)(2,1)}) %reduce-scatter.28.cloned.1.call-update) | async-done | bytes 1048592 | tf_op jit(solution)/shard_map/reduce_scatter | solution.py:240
  1164.4 147.7 %reduce-scatter.32.cloned.1.call-done = bf16[2048,256]{1,0:T(8,128)(2,1)} async-done(((bf16[2048,2048]{1,0:T(8,128)(2,1)}), bf16[2048,256]{1,0:T(8,128)(2,1)}) %reduce-scatter.32.cloned.1.call-update) | async-done | bytes 1048592 | tf_op jit(solution)/shard_map/reduce_scatter | solution.py:246
  1314.8 62.8 %reduce-scatter.24.cloned.1.call-done = bf16[256,128]{1,0:T(8,128)(2,1)} async-done(((bf16[2048,128]{1,0:T(8,128)(2,1)}), bf16[256,128]{1,0:T(8,128)(2,1)}) %reduce-scatter.24.cloned.1.call-update) | async-done | bytes 65552 | tf_op jit(solution)/shard_map/reduce_scatter | solution.py:298
  1379.1 63.9 %reduce-scatter.22.cloned.1.call-done = bf16[256,128]{1,0:T(8,128)(2,1)} async-done(((bf16[2048,128]{1,0:T(8,128)(2,1)}), bf16[256,128]{1,0:T(8,128)(2,1)}) %reduce-scatter.22.cloned.1.call-update) | async-done | bytes 65552 | tf_op jit(solution)/shard_map/reduce_scatter | solution.py:295
  1444.5 69.8 %reduce-scatter.26.cloned.1.call-done = bf16[512,256]{1,0:T(8,128)(2,1)} async-done(((bf16[512,2048]{1,0:T(8,128)(2,1)}), bf16[512,256]{1,0:T(8,128)(2,1)}) %reduce-scatter.26.cloned.1.call-update) | async-done | bytes 262160 | tf_op jit(solution)/shard_map/reduce_scatter | solution.py:301
  1516.1 69.0 %reduce-scatter.20.cloned.1.call-done = bf16[256,512]{1,0:T(8,128)(2,1)} async-done(((bf16[2048,512]{1,0:T(8,128)(2,1)}), bf16[256,512]{1,0:T(8,128)(2,1)}) %reduce-scatter.20.cloned.1.call-update) | async-done | bytes 262160 | tf_op jit(solution)/shard_map/reduce_scatter | solution.py:292
  1586.9 44.3 %reduce-scatter.18.cloned.1.call-done = bf16[256,2048]{1,0:T(8,128)(2,1)} async-done(((bf16[1024,2048]{1,0:T(8,128)(2,1)}), bf16[256,2048]{1,0:T(8,128)(2,1)}) %reduce-scatter.18.cloned.1.call-update) | async-done | bytes 1048592 | tf_op jit(solution)/shard_map/reduce_scatter | solution.py:272
  1633.3 21.7 %all-reduce.3 = (bf16[2048]{0:T(1024)(128)(2,1)S(1)}, bf16[2048]{0:T(1024)(128)(2,1)S(1)}) all-reduce(bf16[2048]{0:T(1024)(128)(2,1)S(1)} %get-tuple-element.13, bf16[2048]{0:T(1024)(128)(2,1)S(1)} %copy-done.53), channel_id=6, replica_groups=mesh['dp'=8,'tensor'=4] {'dp'}, use_global_device_ids=true, to_apply=%region_15.16.clone | all-reduce | flops 4096 | bytes 16384
  1655.2 7.0 all-reduce.2
  1662.2 16.2 reduce-scatter.14.cloned.1.call-done
  1678.4 5.3 fusion.25
  (254 shorter events, 100.6 us)
Async XLA Ops:
  7.2 27.9 %copy-start.34 = (f32[256,512]{1,0:T(8,128)S(1)}, f32[256,512]{1,0:T(8,128)}, u32[]{:S(2)}) copy-start(f32[256,512]{1,0:T(8,128)} %param.18) | copy-start | bytes 1572868
  7.2 28.7 %copy-start.35 = (f32[512,256]{1,0:T(8,128)S(1)}, f32[512,256]{1,0:T(8,128)}, u32[]{:S(2)}) copy-start(f32[512,256]{1,0:T(8,128)} %param.21) | copy-start | bytes 1572868
  7.2 29.5 %copy-start.50 = (s32[1024]{0:T(1024)S(1)}, s32[1024]{0:T(1024)}, u32[]{:S(2)}) copy-start(s32[1024]{0:T(1024)} %param.14) | copy-start | bytes 12292
  7.2 29.5 %copy-start.58 = (s32[1024]{0:T(1024)S(1)}, s32[1024]{0:T(1024)}, u32[]{:S(2)}) copy-start(s32[1024]{0:T(1024)} %param.15) | copy-start | bytes 12292
  7.2 29.6 %copy-start.42 = (f32[256,128]{1,0:T(8,128)S(1)}, f32[256,128]{1,0:T(8,128)}, u32[]{:S(2)}) copy-start(f32[256,128]{1,0:T(8,128)} %param.19) | copy-start | bytes 393220
  7.2 29.6 %copy-start.43 = (f32[256,128]{1,0:T(8,128)S(1)}, f32[256,128]{1,0:T(8,128)}, u32[]{:S(2)}) copy-start(f32[256,128]{1,0:T(8,128)} %param.20) | copy-start | bytes 393220
  7.2 96.2 %all-gather.12.cloned.1.call-start = ((), (), s32[]{:S(2)}) async-start(), calls=%async_computation.11 | async-start | bytes 5242880 | tf_op jit(solution)/shard_map/all_gather | solution.py:136
  9.6 27.2 %copy-start.54 = (f32[256]{0:T(256)}, f32[256]{0:T(256)S(1)}, u32[]{:S(2)}) copy-start(f32[256]{0:T(256)S(1)} %add_rsqrt_fusion.1) | copy-start | bytes 3076
  35.0 84.7 %all-gather.14.cloned.1.call-start = ((), (), s32[]{:S(2)}) async-start(), calls=%async_computation.12 | async-start | bytes 2359296 | tf_op jit(solution)/shard_map/all_gather | solution.py:160
  35.8 137.6 %all-gather.16.cloned.1.call-start = ((), (), s32[]{:S(2)}) async-start(), calls=%async_computation.13 | async-start | bytes 2359296 | tf_op jit(solution)/shard_map/all_gather | solution.py:163
  36.6 214.8 %reduce-scatter.12.cloned.1.call-start = ((), (), s32[]{:S(2)}) async-start(), calls=%async_computation.14 | async-start | bytes 10485760 | tf_op jit(solution)/shard_map/reduce_scatter | solution.py:193
  68.3 72.8 %copy-start.14 = (bf16[2048,128]{1,0:T(8,128)(2,1)}, bf16[2048,128]{1,0:T(8,128)(2,1)S(1)}, u32[]{:S(2)}) copy-start(bf16[2048,128]{1,0:T(8,128)(2,1)S(1)} %all_gather.50) | copy-start | bytes 1572868
  100.7 24.3 %copy-start.16 = (bf16[2048,128]{1,0:T(8,128)(2,1)}, bf16[2048,128]{1,0:T(8,128)(2,1)S(1)}, u32[]{:S(2)}) copy-start(bf16[2048,128]{1,0:T(8,128)(2,1)S(1)} %all_gather.51) | copy-start | bytes 1572868
  107.2 42.9 %copy-start.22 = (bf16[1024,2,32]{0,2,1:T(8,128)(2,1)}, bf16[1024,2,32]{0,2,1:T(8,128)(2,1)S(1)}, u32[]{:S(2)}) copy-start(bf16[1024,2,32]{0,2,1:T(8,128)(2,1)S(1)} %get-tuple-element.36) | copy-start | bytes 393220
  107.3 42.9 %copy-start.24 = (bf16[1024,2,32]{0,2,1:T(8,128)(2,1)}, bf16[1024,2,32]{0,2,1:T(8,128)(2,1)S(1)}, u32[]{:S(2)}) copy-start(bf16[1024,2,32]{0,2,1:T(8,128)(2,1)S(1)} %get-tuple-element.37) | copy-start | bytes 393220
  125.4 24.8 %copy-start.18 = (bf16[512,8,64]{0,2,1:T(8,128)(2,1)}, bf16[512,8,64]{0,2,1:T(8,128)(2,1)S(1)}, u32[]{:S(2)}) copy-start(bf16[512,8,64]{0,2,1:T(8,128)(2,1)S(1)} %get-tuple-element.32) | copy-start | bytes 1572868
  142.6 23.2 %copy-start.26 = (bf16[1024,128]{0,1:T(8,128)(2,1)}, bf16[1024,128]{0,1:T(8,128)(2,1)S(1)}, u32[]{:S(2)}) copy-start(bf16[1024,128]{0,1:T(8,128)(2,1)S(1)} %convolution_convert_fusion.9) | copy-start | bytes 786436
  181.2 70.2 %copy-start.4 = (bf16[256,2048]{1,0:T(8,128)(2,1)S(1)}, bf16[256,2048]{1,0:T(8,128)(2,1)}, u32[]{:S(2)}) copy-start(bf16[256,2048]{1,0:T(8,128)(2,1)} %param.13) | copy-start | bytes 3145732
  181.2 197.3 %all-gather.22.cloned.1.call-start = ((), (), s32[]{:S(2)}) async-start(), calls=%async_computation.17 | async-start | bytes 9437184 | tf_op jit(solution)/shard_map/all_gather | solution.py:168
  183.9 229.3 %all-gather.18.cloned.1.call-start = ((), (), s32[]{:S(2)}) async-start(), calls=%async_computation.15 | async-start | bytes 5242880 | tf_op jit(solution)/shard_map/all_gather | solution.py:136
  202.3 621.2 %copy-start.36 = (f32[8,1,256]{2,1,0:T(1,128)}, f32[8,1,256]{2,1,0:T(1,128)S(1)}, u32[]{:S(2)}) copy-start(f32[8,1,256]{2,1,0:T(1,128)S(1)} %convert_element_type.254) | copy-start | bytes 24580
  253.4 570.1 %copy-start.2 = (f32[256,2048]{1,0:T(8,128)}, f32[256,2048]{1,0:T(8,128)S(1)}, u32[]{:S(2)}) copy-start(f32[256,2048]{1,0:T(8,128)S(1)} %get-tuple-element.20) | copy-start | bytes 6291460
  253.4 570.1 %copy-start.51 = (f32[256]{0:T(256)}, f32[256]{0:T(256)S(1)}, u32[]{:S(2)}) copy-start(f32[256]{0:T(256)S(1)} %add_rsqrt_fusion) | copy-start | bytes 3076
  254.9 285.5 %all-gather.20.cloned.1.call-start = ((), (), s32[]{:S(2)}) async-start(), calls=%async_computation.16 | async-start | bytes 9437184 | tf_op jit(solution)/shard_map/all_gather | solution.py:167
  257.6 316.9 %all-gather.26.cloned.1.call-start = ((), (), s32[]{:S(2)}) async-start(), calls=%async_computation.20 | async-start | bytes 5242880 | tf_op jit(solution)/shard_map/all_gather | solution.py:140
  258.4 443.8 %all-gather.24.cloned.1.call-start = ((), (), s32[]{:S(2)}) async-start(), calls=%async_computation.18 | async-start | bytes 9437184 | tf_op jit(solution)/shard_map/all_gather | solution.py:169
  261.1 559.4 %reduce-scatter.16.cloned.1.call-start = ((), (), s32[]{:S(2)}) async-start(), calls=%async_computation.21 | async-start | bytes 10485760 | tf_op jit(solution)/shard_map/reduce_scatter | solution.py:228
  750.8 73.2 %copy-start.11 = (bf16[256,2048]{1,0:T(8,128)(2,1)S(1)}, bf16[256,2048]{1,0:T(8,128)(2,1)}, u32[]{:S(2)}) copy-start(bf16[256,2048]{1,0:T(8,128)(2,1)} %param.16) | copy-start | bytes 3145732
  750.8 118.5 %all-gather.28.cloned.1.call-start = ((), (), s32[]{:S(2)}) async-start(), calls=%async_computation.22 | async-start | bytes 5242880 | tf_op jit(solution)/shard_map/all_gather | solution.py:140
  825.7 185.7 %reduce-scatter.30.cloned.1.call-start = ((), (), s32[]{:S(2)}) async-start(), calls=%async_computation.29 | async-start | bytes 9437184 | tf_op jit(solution)/shard_map/reduce_scatter | solution.py:243
  840.0 321.5 %reduce-scatter.28.cloned.1.call-start = ((), (), s32[]{:S(2)}) async-start(), calls=%async_computation.28 | async-start | bytes 9437184 | tf_op jit(solution)/shard_map/reduce_scatter | solution.py:240
  854.2 457.8 %reduce-scatter.32.cloned.1.call-start = ((), (), s32[]{:S(2)}) async-start(), calls=%async_computation.30 | async-start | bytes 9437184 | tf_op jit(solution)/shard_map/reduce_scatter | solution.py:246
  868.6 509.0 %reduce-scatter.24.cloned.1.call-start = ((), (), s32[]{:S(2)}) async-start(), calls=%async_computation.26 | async-start | bytes 589824 | tf_op jit(solution)/shard_map/reduce_scatter | solution.py:298
  894.8 33.4 %slice-start = ((s8[16777216]{0:T(1024)(128)(4,1)}), s8[4194304]{0:T(1024)(128)(4,1)S(1)}, s32[]{:S(2)}) async-start(s8[16777216]{0:T(1024)(128)(4,1)} %bitcast.151), calls=%async_computation.31 | async-start | bytes 8388608
  894.8 33.4 %slice-start.1 = ((s8[16777216]{0:T(1024)(128)(4,1)}), s8[4194304]{0:T(1024)(128)(4,1)S(1)}, s32[]{:S(2)}) async-start(s8[16777216]{0:T(1024)(128)(4,1)} %bitcast.151), calls=%async_computation.32 | async-start | bytes 8388608
  935.9 507.1 %reduce-scatter.22.cloned.1.call-start = ((), (), s32[]{:S(2)}) async-start(), calls=%async_computation.25 | async-start | bytes 589824 | tf_op jit(solution)/shard_map/reduce_scatter | solution.py:295
  955.8 558.5 %reduce-scatter.26.cloned.1.call-start = ((), (), s32[]{:S(2)}) async-start(), calls=%async_computation.27 | async-start | bytes 2359296 | tf_op jit(solution)/shard_map/reduce_scatter | solution.py:301
  961.8 623.3 %reduce-scatter.20.cloned.1.call-start = ((), (), s32[]{:S(2)}) async-start(), calls=%async_computation.24 | async-start | bytes 2359296 | tf_op jit(solution)/shard_map/reduce_scatter | solution.py:292
  978.6 652.7 %reduce-scatter.18.cloned.1.call-start = ((), (), s32[]{:S(2)}) async-start(), calls=%async_computation.23 | async-start | bytes 5242880 | tf_op jit(solution)/shard_map/reduce_scatter | solution.py:272
  986.2 692.2 %reduce-scatter.14.cloned.1.call-start = ((), (), s32[]{:S(2)}) async-start(), calls=%async_computation.19 | async-start | bytes 5242880 | tf_op jit(solution)/shard_map/reduce_scatter | solution.py:203
  1014.2 617.1 %copy-start.5 = (bf16[256,2048]{1,0:T(8,128)(2,1)S(1)}, bf16[256,2048]{1,0:T(8,128)(2,1)}, u32[]{:S(2)}) copy-start(bf16[256,2048]{1,0:T(8,128)(2,1)} %param.13) | copy-start | bytes 3145732
  1014.2 617.1 %copy-start.45 = (f32[8,1,256]{2,1,0:T(1,128)S(1)}, f32[8,1,256]{2,1,0:T(1,128)}, u32[]{:S(2)}) copy-start(f32[8,1,256]{2,1,0:T(1,128)} %copy-done.44) | copy-start | bytes 24580
  1014.2 617.1 %copy-start.55 = (f32[256]{0:T(256)S(1)}, f32[256]{0:T(256)}, u32[]{:S(2)}) copy-start(f32[256]{0:T(256)} %copy-done.54) | copy-start | bytes 3076
  1164.4 468.9 %copy-start.53 = (bf16[2048]{0:T(1024)(128)(2,1)S(1)}, bf16[2048]{0:T(1024)(128)(2,1)}, u32[]{:S(2)}) copy-start(bf16[2048]{0:T(1024)(128)(2,1)} %get-tuple-element.11) | copy-start | bytes 12292
  1164.4 514.0 %copy-start.3 = (f32[256,2048]{1,0:T(8,128)S(1)}, f32[256,2048]{1,0:T(8,128)}, u32[]{:S(2)}) copy-start(f32[256,2048]{1,0:T(8,128)} %copy-done.2) | copy-start | bytes 6291460
  1164.4 514.0 %copy-start.37 = (f32[8,1,256]{2,1,0:T(1,128)S(1)}, f32[8,1,256]{2,1,0:T(1,128)}, u32[]{:S(2)}) copy-start(f32[8,1,256]{2,1,0:T(1,128)} %copy-done.36) | copy-start | bytes 24580
  1164.4 514.0 %copy-start.52 = (f32[256]{0:T(256)S(1)}, f32[256]{0:T(256)}, u32[]{:S(2)}) copy-start(f32[256]{0:T(256)} %copy-done.51) | copy-start | bytes 3076
  1164.4 514.0 %copy-start.57 = (f32[256]{0:T(256)S(1)}, f32[256]{0:T(256)}, u32[]{:S(2)}) copy-start(f32[256]{0:T(256)} %copy-done.56) | copy-start | bytes 3076
  (44 other events, 273.8 us)
Sparse Core Ops, SparseCore 0:
  35.1 31.7 all-gather.11
  69.6 50.0 all-gather.13
  122.3 48.8 all-gather.15
  181.3 70.0 reduce-scatter.11
  254.0 124.4 all-gather.21
  380.5 32.6 all-gather.17
  415.8 124.4 all-gather.19
  541.9 32.6 all-gather.25
  577.2 124.9 all-gather.23
  750.9 69.5 reduce-scatter.15
  825.8 34.4 all-gather.27
  863.8 147.5 reduce-scatter.29
  1015.0 146.5 reduce-scatter.27
  1165.1 146.9 reduce-scatter.31
  1315.8 61.7 reduce-scatter.23
  1381.4 61.5 reduce-scatter.21
  1446.4 67.8 reduce-scatter.25
  1517.7 67.3 reduce-scatter.19
  1587.6 43.5 reduce-scatter.17
  1633.6 44.7 reduce-scatter.13
where the time goes:
time: 1700 us; the launch traced here: 1690 us
  waiting for transfers between devices  1170 us (69%)
  matrix products  263 us (15%)
  blocking collectives  133 us (8%)
  other arithmetic  87.9 us (5%)
    reduce_scatter x1, waiting for transfers between devices, local(): lax.psum_scatter(grad_w_down.astype(jnp.bfloat16), 'dp', scatter_dimensio...  148 us
    reduce_scatter x1, waiting for transfers between devices, local(): lax.psum_scatter(grad_w_gate.astype(jnp.bfloat16), 'dp', scatter_dimensio...  147 us
    all_gather x1, waiting for transfers between devices, local(): lax.all_gather(w_down.astype(jnp.bfloat16), 'dp', axis=1, tiled=True)  128 us
    all_gather x1, waiting for transfers between devices, local(): lax.all_gather(w_up.astype(jnp.bfloat16), 'dp', axis=0, tiled=True)  117 us
    all_gather x1, waiting for transfers between devices, local(): lax.all_gather(w_gate.astype(jnp.bfloat16), 'dp', axis=0, tiled=True)  112 us
    reduce_scatter x1, waiting for transfers between devices, local(): lax.psum_scatter(grad_w_out.astype(jnp.bfloat16), 'dp', scatter_dimension...  69.8 us
    reduce_scatter x1, waiting for transfers between devices, local(): lax.psum_scatter(back_product((grad_gate, grad_up), (gate_weight, up_weig...  69.7 us
    reduce_scatter x1, waiting for transfers between devices, local(): lax.psum_scatter(grad_w_query.astype(jnp.bfloat16), 'dp', scatter_dimensi...  69 us
  transfers between devices with their start and end apart: 20, of which 17 were waited for; matrix products, arithmetic and copies ran while one was open for 17% of the time, Pallas kernels for 0%

commit v1 on v0

--- a/solution.py
+++ b/solution.py
@@ -8,6 +8,28 @@
 HEADS = 32
 KV_HEADS = 8
 HEAD_DIM = 64
+
+
+def laid_out(blocks, dim):
+    blocks = jnp.moveaxis(blocks, 0, dim)
+    dims = blocks.shape
+    return blocks.reshape(*dims[:dim], dims[dim] * dims[dim + 1], *dims[dim + 2 :])
+
+
+def doubled(value, axis):
+    size = lax.axis_size(axis)
+    tiles = value[None]
+    for level in range(size.bit_length() - 1):
+        bit = 1 << level
+        partner_block = lax.ppermute(tiles, axis, [(i, i ^ bit) for i in range(size)])
+        both = jnp.stack([tiles, partner_block])
+        upper = lax.axis_index(axis) >> level & 1
+        tiles = jnp.where(upper == 0, both, both[::-1]).reshape(-1, *value.shape)
+    return tiles
+
+
+def collect(x, axis, dim):
+    return laid_out(doubled(x, axis), dim)
 
 
 def rotary_angles(positions, head_size):
@@ -165,7 +187,7 @@
     mlp_gain, gate_weight, up_weight, down_weight = (
         lax.all_gather(mlp_norm.astype(jnp.bfloat16), "dp", axis=0, tiled=True),
         lax.all_gather(w_gate.astype(jnp.bfloat16), "dp", axis=0, tiled=True),
-        lax.all_gather(w_up.astype(jnp.bfloat16), "dp", axis=0, tiled=True),
+        collect(w_up.astype(jnp.bfloat16), "dp", 0),
         lax.all_gather(w_down.astype(jnp.bfloat16), "dp", axis=1, tiled=True),
     )
     group = HEADS // KV_HEADS

time: 1700 us -> 1840 us (1.082)
  waiting for transfers between devices: 1170 us -> 1280 us
  other arithmetic: 87.9 us -> 122 us
    ppermute x0 -> x3, waiting for transfers between devices: none -> 427 us  [doubled(): lax.ppermute(tiles, axis, [(i, i ^ bit) for i in range(size)])]
    reduce_scatter x1, waiting for transfers between devices: 9.3 us -> 147 us  [local(): lax.psum_scatter(grad_w_up.astype(jnp.bfloat16), 'dp', scatter_dimension=...]
    reduce_scatter x1, waiting for transfers between devices: 147 us -> 15.9 us  [local(): lax.psum_scatter(grad_w_gate.astype(jnp.bfloat16), 'dp', scatter_dimensio...]
    all_gather x1, waiting for transfers between devices: 128 us -> 0.01 us  [local(): lax.all_gather(w_down.astype(jnp.bfloat16), 'dp', axis=1, tiled=True)]
    all_gather x1, waiting for transfers between devices: 112 us -> 0.01 us  [local(): lax.all_gather(w_gate.astype(jnp.bfloat16), 'dp', axis=0, tiled=True)]
    all_gather x1, waiting for transfers between devices: 117 us -> 77.1 us  [local(): lax.all_gather(w_up.astype(jnp.bfloat16), 'dp', axis=0, tiled=True)]
    all_gather x2, waiting for transfers between devices: 19.7 us -> 0.02 us  [gather_grads(): return lax.all_gather(rows, 'tensor', axis=0, tiled=True)]
  transfers between devices with their start and end apart: 20 -> 23, of which waited for: 17 -> 17; matrix products, arithmetic and copies ran while one was open for 17% -> 19% of each run, Pallas kernels for 0% -> 0%
where the time goes in v1:
time: 1840 us; the launch traced here: 1830 us
  waiting for transfers between devices  1280 us (70%)
  matrix products  260 us (14%)
  blocking collectives  136 us (7%)
  other arithmetic  122 us (7%)
    ppermute x3, waiting for transfers between devices, doubled(): lax.ppermute(tiles, axis, [(i, i ^ bit) for i in range(size)])  427 us
    reduce_scatter x1, waiting for transfers between devices, local(): lax.psum_scatter(grad_w_down.astype(jnp.bfloat16), 'dp', scatter_dimensio...  148 us
    reduce_scatter x1, waiting for transfers between devices, local(): lax.psum_scatter(grad_w_up.astype(jnp.bfloat16), 'dp', scatter_dimension=...  147 us
    all_gather x1, waiting for transfers between devices, local(): lax.all_gather(w_up.astype(jnp.bfloat16), 'dp', axis=0, tiled=True)  77.1 us
    reduce_scatter x1, waiting for transfers between devices, local(): lax.psum_scatter(back_product((grad_gate, grad_up), (gate_weight, up_weig...  69.7 us
    reduce_scatter x1, waiting for transfers between devices, local(): lax.psum_scatter(grad_w_query.astype(jnp.bfloat16), 'dp', scatter_dimensi...  69.6 us
    reduce_scatter x1, waiting for transfers between devices, local(): lax.psum_scatter(grad_w_out.astype(jnp.bfloat16), 'dp', scatter_dimension...  69.6 us
    reduce_scatter x1, waiting for transfers between devices, local(): lax.psum_scatter(grad_w_key.astype(jnp.bfloat16), 'dp', scatter_dimension...  64 us
  transfers between devices with their start and end apart: 23, of which 17 were waited for; matrix products, arithmetic and copies ran while one was open for 19% of the time, Pallas kernels for 0%

profile of v1, /device:TPU:0, one launch (start us, length us, event | category | flops | bytes accessed | tf_op | source)
XLA Modules:
  0.0 1830.9 jit_solution(4559965967047282567)
XLA Ops:
  9.9 22.3 %all-gather = bf16[8,1,256]{2,1,0:T(2,128)(2,1)S(1)} all-gather(bf16[1,1,256]{2,1,0:T(2,128)(2,1)S(1)} %reshape.235), channel_id=1, replica_groups=mesh['dp'=8,'tensor'=4] {'dp'}, dimensions={0}, use_global_device_ids=true | all-gather | bytes 4608 | tf_op jit(solution)/shard_map/all_gather | solution.py:181
  37.2 33.3 %all_gather.50 = bf16[2048,128]{1,0:T(8,128)(2,1)S(1)} all-gather(bf16[256,128]{1,0:T(8,128)(2,1)S(1)} %convert_element_type.200), channel_id=1, replica_groups=mesh['dp'=8,'tensor'=4] {'dp'}, dimensions={0}, use_global_device_ids=true | all-gather | bytes 589824 | tf_op jit(solution)/shard_map/all_gather | solution.py:183
  70.6 31.3 %all_gather.49 = bf16[2048,128]{1,0:T(8,128)(2,1)S(1)} all-gather(bf16[256,128]{1,0:T(8,128)(2,1)S(1)} %convert_element_type.198), channel_id=1, replica_groups=mesh['dp'=8,'tensor'=4] {'dp'}, dimensions={0}, use_global_device_ids=true | all-gather | bytes 589824 | tf_op jit(solution)/shard_map/all_gather | solution.py:184
  105.3 5.4 fusion.64
  113.6 7.3 fusion.62
  120.9 8.1 fusion.6
  130.6 7.6 fusion.47
  138.2 7.5 fusion.61
  145.7 8.1 fusion.7
  153.9 7.4 fusion.48
  161.5 7.7 fusion.65
  174.7 20.6 %all-gather.1 = bf16[8,1,256]{2,1,0:T(2,128)(2,1)S(1)} all-gather(bf16[1,1,256]{2,1,0:T(2,128)(2,1)S(1)} %reshape.237), channel_id=1, replica_groups=mesh['dp'=8,'tensor'=4] {'dp'}, dimensions={0}, use_global_device_ids=true | all-gather | bytes 4608 | tf_op jit(solution)/shard_map/all_gather | solution.py:188
  195.3 45.5 %reduce-scatter.12.cloned.1.call-done = f32[256,2048]{1,0:T(8,128)} async-done(((f32[1024,2048]{1,0:T(8,128)}), f32[256,2048]{1,0:T(8,128)}) %reduce-scatter.12.cloned.1.call-update) | async-done | bytes 2097168 | tf_op jit(solution)/shard_map/reduce_scatter | solution.py:215
  249.5 21.5 %collective-permute-done = bf16[1,256,2048]{2,1,0:T(8,128)(2,1)} collective-permute-done((bf16[1,256,2048]{2,1,0:T(8,128)(2,1)S(1)}, bf16[1,256,2048]{2,1,0:T(8,128)(2,1)}, u32[]{:S(2)}, u32[]{:S(2)}) %collective-permute-start) | collective-permute-done | bytes 1048608 | tf_op jit(solution)/shard_map/ppermute | solution.py:24
  278.2 77.3 %collective-permute-done.1 = bf16[2,256,2048]{2,1,0:T(8,128)(2,1)} collective-permute-done((bf16[2,256,2048]{2,1,0:T(8,128)(2,1)}, bf16[2,256,2048]{2,1,0:T(8,128)(2,1)}, u32[]{:S(2)}, u32[]{:S(2)}) %collective-permute-start.1) | collective-permute-done | bytes 2097184 | tf_op jit(solution)/shard_map/ppermute | solution.py:24
  362.9 327.8 %collective-permute-done.2 = bf16[4,256,2048]{2,1,0:T(8,128)(2,1)} collective-permute-done((bf16[4,256,2048]{2,1,0:T(8,128)(2,1)}, bf16[4,256,2048]{2,1,0:T(8,128)(2,1)}, u32[]{:S(2)}, u32[]{:S(2)}) %collective-permute-start.2) | collective-permute-done | bytes 4194336 | tf_op jit(solution)/shard_map/ppermute | solution.py:24
  690.7 7.6 pad_maximum_fusion
  698.3 14.3 reverse_select_fusion
  712.6 14.8 fusion.67
  727.4 20.5 %all-gather.18.cloned.1.call-done = bf16[1024,2048]{1,0:T(8,128)(2,1)} async-done(((bf16[256,2048]{1,0:T(8,128)(2,1)}), bf16[1024,2048]{1,0:T(8,128)(2,1)}) %all-gather.18.cloned.1.call-update) | async-done | bytes 4194320 | tf_op jit(solution)/shard_map/all_gather | solution.py:158
  747.9 15.5 fusion.66
  763.4 19.3 %multiply_convert_fusion = (bf16[1024,2048]{1,0:T(8,128)(2,1)}, bf16[1024,2048]{1,0:T(8,128)(2,1)}, bf16[1024,2048]{1,0:T(8,128)(2,1)}) fusion(f32[1024,2048]{1,0:T(8,128)} %fusion.67, f32[1024,2048]{1,0:T(8,128)} %fusion.66, bf16[1024,2048]{1,0:T(8,128)(2,1)S(1)} %copy-done.58, bf16[2048,2048]{1,0:T(8,128)(2,1)} %bitcast.167), kind=kOutput, calls=%fused_computation.29 | convolution fusion | flops 8621391872 | bytes 41943040 | tf_op jit(solution)/shard_map/dot_general | solution.py:221
  782.7 14.7 fusion.68
  797.5 77.1 %all-gather.26.cloned.1.call-done = bf16[2048,2048]{1,0:T(8,128)(2,1)} async-done(((bf16[256,2048]{1,0:T(8,128)(2,1)}), bf16[2048,2048]{1,0:T(8,128)(2,1)}) %all-gather.26.cloned.1.call-update) | async-done | bytes 8388624 | tf_op jit(solution)/shard_map/all_gather | solution.py:235
  874.6 15.7 convolution_add_fusion
  890.3 69.7 %reduce-scatter.16.cloned.1.call-done = f32[256,2048]{1,0:T(8,128)} async-done(((f32[1024,2048]{1,0:T(8,128)}), f32[256,2048]{1,0:T(8,128)}) %reduce-scatter.16.cloned.1.call-update) | async-done | bytes 2097168 | tf_op jit(solution)/shard_map/reduce_scatter | solution.py:250
  965.2 14.3 convolution_convert_fusion.2
  979.6 14.1 convolution_convert_fusion.1
  993.8 14.6 convolution_convert_fusion
  1015.0 11.0 fusion
  1026.0 12.3 fusion.2
  1045.2 7.6 fusion.3
  1052.9 10.7 fusion.5
  1063.6 6.2 fusion.46
  1073.0 8.9 fusion.52
  1105.1 5.9 convolution_convert_fusion.4
  1119.0 13.9 convolution_convert_fusion.3
  1134.8 15.9 reduce-scatter.28.cloned.1.call-done
  1153.5 147.5 %reduce-scatter.30.cloned.1.call-done = bf16[256,2048]{1,0:T(8,128)(2,1)} async-done(((bf16[2048,2048]{1,0:T(8,128)(2,1)}), bf16[256,2048]{1,0:T(8,128)(2,1)}) %reduce-scatter.30.cloned.1.call-update) | async-done | bytes 1048592 | tf_op jit(solution)/shard_map/reduce_scatter | solution.py:265
  1303.7 147.6 %reduce-scatter.32.cloned.1.call-done = bf16[2048,256]{1,0:T(8,128)(2,1)} async-done(((bf16[2048,2048]{1,0:T(8,128)(2,1)}), bf16[2048,256]{1,0:T(8,128)(2,1)}) %reduce-scatter.32.cloned.1.call-update) | async-done | bytes 1048592 | tf_op jit(solution)/shard_map/reduce_scatter | solution.py:268
  1454.1 62.9 %reduce-scatter.24.cloned.1.call-done = bf16[256,128]{1,0:T(8,128)(2,1)} async-done(((bf16[2048,128]{1,0:T(8,128)(2,1)}), bf16[256,128]{1,0:T(8,128)(2,1)}) %reduce-scatter.24.cloned.1.call-update) | async-done | bytes 65552 | tf_op jit(solution)/shard_map/reduce_scatter | solution.py:320
  1518.5 64.0 %reduce-scatter.22.cloned.1.call-done = bf16[256,128]{1,0:T(8,128)(2,1)} async-done(((bf16[2048,128]{1,0:T(8,128)(2,1)}), bf16[256,128]{1,0:T(8,128)(2,1)}) %reduce-scatter.22.cloned.1.call-update) | async-done | bytes 65552 | tf_op jit(solution)/shard_map/reduce_scatter | solution.py:317
  1584.0 69.6 %reduce-scatter.20.cloned.1.call-done = bf16[256,512]{1,0:T(8,128)(2,1)} async-done(((bf16[2048,512]{1,0:T(8,128)(2,1)}), bf16[256,512]{1,0:T(8,128)(2,1)}) %reduce-scatter.20.cloned.1.call-update) | async-done | bytes 262160 | tf_op jit(solution)/shard_map/reduce_scatter | solution.py:314
  1655.4 69.6 %reduce-scatter.26.cloned.1.call-done = bf16[512,256]{1,0:T(8,128)(2,1)} async-done(((bf16[512,2048]{1,0:T(8,128)(2,1)}), bf16[512,256]{1,0:T(8,128)(2,1)}) %reduce-scatter.26.cloned.1.call-update) | async-done | bytes 262160 | tf_op jit(solution)/shard_map/reduce_scatter | solution.py:323
  1726.7 44.4 %reduce-scatter.18.cloned.1.call-done = bf16[256,2048]{1,0:T(8,128)(2,1)} async-done(((bf16[1024,2048]{1,0:T(8,128)(2,1)}), bf16[256,2048]{1,0:T(8,128)(2,1)}) %reduce-scatter.18.cloned.1.call-update) | async-done | bytes 1048592 | tf_op jit(solution)/shard_map/reduce_scatter | solution.py:294
  1773.2 21.7 %all-reduce.3 = (bf16[2048]{0:T(1024)(128)(2,1)S(1)}, bf16[2048]{0:T(1024)(128)(2,1)S(1)}) all-reduce(bf16[2048]{0:T(1024)(128)(2,1)S(1)} %get-tuple-element.13, bf16[2048]{0:T(1024)(128)(2,1)S(1)} %copy-done.52), channel_id=6, replica_groups=mesh['dp'=8,'tensor'=4] {'dp'}, use_global_device_ids=true, to_apply=%region_15.16.clone | all-reduce | flops 4096 | bytes 16384
  1795.1 7.0 all-reduce.2
  1802.1 16.2 reduce-scatter.14.cloned.1.call-done
  (257 shorter events, 120.9 us)
Async XLA Ops:
  7.2 29.1 %copy-start.34 = (f32[512,256]{1,0:T(8,128)S(1)}, f32[512,256]{1,0:T(8,128)}, u32[]{:S(2)}) copy-start(f32[512,256]{1,0:T(8,128)} %param.21) | copy-start | bytes 1572868
  7.2 30.0 %copy-start.49 = (s32[1024]{0:T(1024)S(1)}, s32[1024]{0:T(1024)}, u32[]{:S(2)}) copy-start(s32[1024]{0:T(1024)} %param.14) | copy-start | bytes 12292
  7.2 30.0 %copy-start.57 = (s32[1024]{0:T(1024)S(1)}, s32[1024]{0:T(1024)}, u32[]{:S(2)}) copy-start(s32[1024]{0:T(1024)} %param.15) | copy-start | bytes 12292
  7.2 30.0 %copy-start.41 = (f32[256,128]{1,0:T(8,128)S(1)}, f32[256,128]{1,0:T(8,128)}, u32[]{:S(2)}) copy-start(f32[256,128]{1,0:T(8,128)} %param.19) | copy-start | bytes 393220
  7.2 63.4 %copy-start.42 = (f32[256,128]{1,0:T(8,128)S(1)}, f32[256,128]{1,0:T(8,128)}, u32[]{:S(2)}) copy-start(f32[256,128]{1,0:T(8,128)} %param.20) | copy-start | bytes 393220
  7.2 97.4 %all-gather.14.cloned.1.call-start = ((), (), s32[]{:S(2)}) async-start(), calls=%async_computation.12 | async-start | bytes 2359296 | tf_op jit(solution)/shard_map/all_gather | solution.py:182
  9.1 96.2 %all-gather.12.cloned.1.call-start = ((), (), s32[]{:S(2)}) async-start(), calls=%async_computation.11 | async-start | bytes 5242880 | tf_op jit(solution)/shard_map/all_gather | solution.py:158
  33.7 70.9 %copy-start.53 = (f32[256]{0:T(256)}, f32[256]{0:T(256)S(1)}, u32[]{:S(2)}) copy-start(f32[256]{0:T(256)S(1)} %add_rsqrt_fusion.1) | copy-start | bytes 3076
  36.3 125.2 %all-gather.16.cloned.1.call-start = ((), (), s32[]{:S(2)}) async-start(), calls=%async_computation.13 | async-start | bytes 2359296 | tf_op jit(solution)/shard_map/all_gather | solution.py:185
  37.1 203.8 %reduce-scatter.12.cloned.1.call-start = ((), (), s32[]{:S(2)}) async-start(), calls=%async_computation.14 | async-start | bytes 10485760 | tf_op jit(solution)/shard_map/reduce_scatter | solution.py:215
  70.6 40.5 %copy-start.13 = (bf16[2048,128]{1,0:T(8,128)(2,1)}, bf16[2048,128]{1,0:T(8,128)(2,1)S(1)}, u32[]{:S(2)}) copy-start(bf16[2048,128]{1,0:T(8,128)(2,1)S(1)} %all_gather.50) | copy-start | bytes 1572868
  101.8 27.1 %copy-start.11 = (bf16[2048,128]{1,0:T(8,128)(2,1)}, bf16[2048,128]{1,0:T(8,128)(2,1)S(1)}, u32[]{:S(2)}) copy-start(bf16[2048,128]{1,0:T(8,128)(2,1)S(1)} %all_gather.49) | copy-start | bytes 1572868
  112.7 25.5 %copy-start.19 = (bf16[1024,2,32]{0,2,1:T(8,128)(2,1)}, bf16[1024,2,32]{0,2,1:T(8,128)(2,1)S(1)}, u32[]{:S(2)}) copy-start(bf16[1024,2,32]{0,2,1:T(8,128)(2,1)S(1)} %get-tuple-element.38) | copy-start | bytes 393220
  112.7 25.5 %copy-start.21 = (bf16[1024,2,32]{0,2,1:T(8,128)(2,1)}, bf16[1024,2,32]{0,2,1:T(8,128)(2,1)S(1)}, u32[]{:S(2)}) copy-start(bf16[1024,2,32]{0,2,1:T(8,128)(2,1)S(1)} %get-tuple-element.39) | copy-start | bytes 393220
  130.5 23.3 %copy-start.23 = (bf16[1024,128]{0,1:T(8,128)(2,1)}, bf16[1024,128]{0,1:T(8,128)(2,1)S(1)}, u32[]{:S(2)}) copy-start(bf16[1024,128]{0,1:T(8,128)(2,1)S(1)} %convolution_convert_fusion.9) | copy-start | bytes 786436
  169.2 543.4 %all-gather.24.cloned.1.call-start = ((), (), s32[]{:S(2)}) async-start(), calls=%async_computation.19 | async-start | bytes 5242880 | tf_op jit(solution)/shard_map/all_gather | solution.py:162
  169.8 71.1 %copy-start.3 = (bf16[256,2048]{1,0:T(8,128)(2,1)S(1)}, bf16[256,2048]{1,0:T(8,128)(2,1)}, u32[]{:S(2)}) copy-start(bf16[256,2048]{1,0:T(8,128)(2,1)} %param.13) | copy-start | bytes 3145732
  169.8 542.8 %all-gather.22.cloned.1.call-start = ((), (), s32[]{:S(2)}) async-start(), calls=%async_computation.17 | async-start | bytes 9437184 | tf_op jit(solution)/shard_map/all_gather | solution.py:191
  171.8 555.6 %all-gather.20.cloned.1.call-start = ((), (), s32[]{:S(2)}) async-start(), calls=%async_computation.16 | async-start | bytes 9437184 | tf_op jit(solution)/shard_map/all_gather | solution.py:189
  174.6 573.3 %all-gather.18.cloned.1.call-start = ((), (), s32[]{:S(2)}) async-start(), calls=%async_computation.15 | async-start | bytes 5242880 | tf_op jit(solution)/shard_map/all_gather | solution.py:158
  195.3 767.6 %copy-start.35 = (f32[8,1,256]{2,1,0:T(1,128)}, f32[8,1,256]{2,1,0:T(1,128)S(1)}, u32[]{:S(2)}) copy-start(f32[8,1,256]{2,1,0:T(1,128)S(1)} %convert_element_type.254) | copy-start | bytes 24580
  242.8 720.1 %copy-start.1 = (f32[256,2048]{1,0:T(8,128)}, f32[256,2048]{1,0:T(8,128)S(1)}, u32[]{:S(2)}) copy-start(f32[256,2048]{1,0:T(8,128)S(1)} %get-tuple-element.20) | copy-start | bytes 6291460
  242.8 720.1 %copy-start.50 = (f32[256]{0:T(256)}, f32[256]{0:T(256)S(1)}, u32[]{:S(2)}) copy-start(f32[256]{0:T(256)S(1)} %add_rsqrt_fusion) | copy-start | bytes 3076
  244.3 630.3 %all-gather.26.cloned.1.call-start = ((), (), s32[]{:S(2)}) async-start(), calls=%async_computation.20 | async-start | bytes 9437184 | tf_op jit(solution)/shard_map/all_gather | solution.py:235
  246.1 24.9 %collective-permute-start = (bf16[1,256,2048]{2,1,0:T(8,128)(2,1)S(1)}, bf16[1,256,2048]{2,1,0:T(8,128)(2,1)}, u32[]{:S(2)}, u32[]{:S(2)}) collective-permute-start(bf16[1,256,2048]{2,1,0:T(8,128)(2,1)S(1)} %convert_bitcast_fusion.1), channel_id=1, source_target_pairs={{0,4},{4,0},{8,12},{12,8},{16,20},{20,16},{24,28},{28,24},{1,5},{5... | collective-permute-start | bytes 3145736 | tf_op jit(solution)/shard_map/ppermute | solution.py:24
  275.1 80.4 %collective-permute-start.1 = (bf16[2,256,2048]{2,1,0:T(8,128)(2,1)}, bf16[2,256,2048]{2,1,0:T(8,128)(2,1)}, u32[]{:S(2)}, u32[]{:S(2)}) collective-permute-start(bf16[2,256,2048]{2,1,0:T(8,128)(2,1)} %get-tuple-element.31), channel_id=1, source_target_pairs={{0,8},{4,12},{8,0},{12,4},{16,24},{20,28},{24,16},{28,20},{1,9},{5... | collective-permute-start | bytes 6291464 | tf_op jit(solution)/shard_map/ppermute | solution.py:24
  277.8 682.3 %reduce-scatter.16.cloned.1.call-start = ((), (), s32[]{:S(2)}) async-start(), calls=%async_computation.21 | async-start | bytes 10485760 | tf_op jit(solution)/shard_map/reduce_scatter | solution.py:250
  361.3 329.5 %collective-permute-start.2 = (bf16[4,256,2048]{2,1,0:T(8,128)(2,1)}, bf16[4,256,2048]{2,1,0:T(8,128)(2,1)}, u32[]{:S(2)}, u32[]{:S(2)}) collective-permute-start(bf16[4,256,2048]{2,1,0:T(8,128)(2,1)} %bitcast.26), channel_id=1, source_target_pairs={{0,16},{4,20},{8,24},{12,28},{16,0},{20,4},{24,8},{28,12},{1,17},{... | collective-permute-start | bytes 12582920 | tf_op jit(solution)/shard_map/ppermute | solution.py:24
  890.3 73.2 %copy-start.10 = (bf16[256,2048]{1,0:T(8,128)(2,1)S(1)}, bf16[256,2048]{1,0:T(8,128)(2,1)}, u32[]{:S(2)}) copy-start(bf16[256,2048]{1,0:T(8,128)(2,1)} %param.16) | copy-start | bytes 3145732
  890.3 118.8 %all-gather.28.cloned.1.call-start = ((), (), s32[]{:S(2)}) async-start(), calls=%async_computation.22 | async-start | bytes 5242880 | tf_op jit(solution)/shard_map/all_gather | solution.py:162
  965.1 185.6 %reduce-scatter.28.cloned.1.call-start = ((), (), s32[]{:S(2)}) async-start(), calls=%async_computation.28 | async-start | bytes 9437184 | tf_op jit(solution)/shard_map/reduce_scatter | solution.py:262
  979.5 321.4 %reduce-scatter.30.cloned.1.call-start = ((), (), s32[]{:S(2)}) async-start(), calls=%async_computation.29 | async-start | bytes 9437184 | tf_op jit(solution)/shard_map/reduce_scatter | solution.py:265
  993.7 457.7 %reduce-scatter.32.cloned.1.call-start = ((), (), s32[]{:S(2)}) async-start(), calls=%async_computation.30 | async-start | bytes 9437184 | tf_op jit(solution)/shard_map/reduce_scatter | solution.py:268
  1008.4 508.6 %reduce-scatter.24.cloned.1.call-start = ((), (), s32[]{:S(2)}) async-start(), calls=%async_computation.26 | async-start | bytes 589824 | tf_op jit(solution)/shard_map/reduce_scatter | solution.py:320
  1026.0 19.2 %slice-start.3 = ((s8[16777216]{0:T(1024)(128)(4,1)}), s8[4194304]{0:T(1024)(128)(4,1)S(1)}, s32[]{:S(2)}) async-start(s8[16777216]{0:T(1024)(128)(4,1)} %bitcast.165), calls=%async_computation.34 | async-start | bytes 8388608
  1084.0 498.5 %reduce-scatter.22.cloned.1.call-start = ((), (), s32[]{:S(2)}) async-start(), calls=%async_computation.25 | async-start | bytes 589824 | tf_op jit(solution)/shard_map/reduce_scatter | solution.py:317
  1098.6 555.0 %reduce-scatter.20.cloned.1.call-start = ((), (), s32[]{:S(2)}) async-start(), calls=%async_computation.24 | async-start | bytes 2359296 | tf_op jit(solution)/shard_map/reduce_scatter | solution.py:314
  1105.0 619.9 %reduce-scatter.26.cloned.1.call-start = ((), (), s32[]{:S(2)}) async-start(), calls=%async_computation.27 | async-start | bytes 2359296 | tf_op jit(solution)/shard_map/reduce_scatter | solution.py:323
  1111.0 660.1 %reduce-scatter.18.cloned.1.call-start = ((), (), s32[]{:S(2)}) async-start(), calls=%async_computation.23 | async-start | bytes 5242880 | tf_op jit(solution)/shard_map/reduce_scatter | solution.py:294
  1118.9 699.3 %reduce-scatter.14.cloned.1.call-start = ((), (), s32[]{:S(2)}) async-start(), calls=%async_computation.18 | async-start | bytes 5242880 | tf_op jit(solution)/shard_map/reduce_scatter | solution.py:225
  1153.5 617.7 %copy-start.4 = (bf16[256,2048]{1,0:T(8,128)(2,1)S(1)}, bf16[256,2048]{1,0:T(8,128)(2,1)}, u32[]{:S(2)}) copy-start(bf16[256,2048]{1,0:T(8,128)(2,1)} %param.13) | copy-start | bytes 3145732
  1153.5 617.7 %copy-start.44 = (f32[8,1,256]{2,1,0:T(1,128)S(1)}, f32[8,1,256]{2,1,0:T(1,128)}, u32[]{:S(2)}) copy-start(f32[8,1,256]{2,1,0:T(1,128)} %copy-done.43) | copy-start | bytes 24580
  1153.5 617.7 %copy-start.54 = (f32[256]{0:T(256)S(1)}, f32[256]{0:T(256)}, u32[]{:S(2)}) copy-start(f32[256]{0:T(256)} %copy-done.53) | copy-start | bytes 3076
  1303.7 469.5 %copy-start.52 = (bf16[2048]{0:T(1024)(128)(2,1)S(1)}, bf16[2048]{0:T(1024)(128)(2,1)}, u32[]{:S(2)}) copy-start(bf16[2048]{0:T(1024)(128)(2,1)} %get-tuple-element.11) | copy-start | bytes 12292
  1303.7 514.5 %copy-start.2 = (f32[256,2048]{1,0:T(8,128)S(1)}, f32[256,2048]{1,0:T(8,128)}, u32[]{:S(2)}) copy-start(f32[256,2048]{1,0:T(8,128)} %copy-done.1) | copy-start | bytes 6291460
  1303.7 514.5 %copy-start.36 = (f32[8,1,256]{2,1,0:T(1,128)S(1)}, f32[8,1,256]{2,1,0:T(1,128)}, u32[]{:S(2)}) copy-start(f32[8,1,256]{2,1,0:T(1,128)} %copy-done.35) | copy-start | bytes 24580
  1303.7 514.5 %copy-start.51 = (f32[256]{0:T(256)S(1)}, f32[256]{0:T(256)}, u32[]{:S(2)}) copy-start(f32[256]{0:T(256)} %copy-done.50) | copy-start | bytes 3076
  1303.7 514.5 %copy-start.56 = (f32[256]{0:T(256)S(1)}, f32[256]{0:T(256)}, u32[]{:S(2)}) copy-start(f32[256]{0:T(256)} %copy-done.55) | copy-start | bytes 3076
  (42 other events, 242.6 us)
Sparse Core Ops, SparseCore 0:
  10.7 57.6 all-gather.13
  70.6 34.6 all-gather.11
  107.9 50.3 all-gather.15
  169.3 71.4 reduce-scatter.11
  242.2 34.4 all-gather.23
  279.2 274.9 all-gather.21
  556.3 156.0 all-gather.19
  714.6 33.2 all-gather.17
  750.1 124.4 all-gather.25
  890.4 69.5 reduce-scatter.15
  965.2 34.4 all-gather.27
  1003.2 147.4 reduce-scatter.27
  1154.3 146.5 reduce-scatter.29
  1304.4 146.8 reduce-scatter.31
  1455.1 61.7 reduce-scatter.23
  1520.7 61.7 reduce-scatter.21
  1585.9 67.6 reduce-scatter.19
  1657.0 67.9 reduce-scatter.25
  1727.5 43.6 reduce-scatter.17
  1773.5 44.7 reduce-scatter.13
